TPU v7x, 32 devices: a whole 2x2x4 slice. The times are simulated.
32 devices in a mesh: row: 8 (over y, x, core), col: 4 (over z).
Axes of the slice: x: 2, y: 2, z: 4, core: 2. Of those that a mesh axis runs over, the one named last changes fastest.
Arguments:
- left_panels: float32 [8, 4, 16, 128, 128], P('row', 'col'), may hold values from -6 to 6
- right_panels: float32 [2, 4, 8, 12, 128, 128], P(None, 'col', 'row'), may hold values from -0.25 to 0.25
- product_lists: int32 [8, 4, 8, 96, 3], P('row', 'col'), may hold values from -1 to 23, as said below
Outputs:
- product_blocks: float32 [8, 4, 24, 128, 128], P('row', 'col')
Inputs may be any that keep to these rules, and one draw needn't show every extreme that they name: `product_lists`: each entry is (left slot < 16, right slot < 12, output slot < 24). In each list the first entries, at least half of 96 and at most 96, are live with distinct (left, right) pairs, the rest are -1 in all three columns; some list holds 96 live entries.
All inputs are finite; a program needn't handle non-finite values.
Results may differ from a plain program's by a relative error of at most 0.0003.
Values sent between devices are 32-bit elements; how exact they have to be, the bound alone decides.
A program may use at most 128 MiB of HBM per device.

v0:
```python
import jax
import jax.numpy as jnp
from jax import lax
from jax.sharding import PartitionSpec as P

BLK = 128
OCAP = 24


def contribute(left_stack, right_panel, entries, slot_count):
    live_mask = entries[:, 0] >= 0
    left_slot = jnp.maximum(entries[:, 0], 0)
    right_slot = jnp.maximum(entries[:, 1], 0)
    taken_left = jnp.take(left_stack, left_slot, axis=0)
    taken_right = jnp.take(right_panel, right_slot, axis=0)
    blocks = jnp.einsum("pik,pkj->pij", taken_left, taken_right, precision=lax.Precision.HIGHEST)
    slot_ids = jnp.arange(slot_count, dtype=jnp.int32)
    onehot = ((entries[:, 2][None, :] == slot_ids[:, None]) & live_mask[None, :]).astype(
        blocks.dtype
    )
    return jnp.einsum("op,pij->oij", onehot, blocks, precision=lax.Precision.HIGHEST)


def shards(left_panels, right_panels, product_lists):
    row_count = lax.axis_size("row")
    col_count = lax.axis_size("col")
    row_pos = lax.axis_index("row")
    col_pos = lax.axis_index("col")
    entries = product_lists[0, 0]
    step_count = entries.shape[0]
    running = jnp.zeros((OCAP, BLK, BLK), jnp.float32)
    right_all = lax.all_gather(right_panels, "col", axis=1, tiled=True)
    pieces = lax.all_gather(left_panels, "row", axis=0, tiled=True)

    def one_row(offset, partial_value):
        step_num = (offset - row_pos - col_pos) % row_count
        left_stack = lax.dynamic_index_in_dim(pieces, offset, 0, keepdims=False)[0]
        right_panel = right_all[offset // col_count, offset % col_count, 0]
        entry_rows = lax.dynamic_index_in_dim(
            entries, jnp.minimum(step_num, step_count - 1), 0, keepdims=False
        )
        return lax.cond(
            step_num < step_count,
            lambda inner: inner + contribute(left_stack, right_panel, entry_rows, OCAP),
            lambda inner: inner,
            partial_value,
        )

    running = lax.fori_loop(0, pieces.shape[0], one_row, running)
    return running[None, None]


def solution(mesh):
    return jax.shard_map(
        shards,
        mesh=mesh,
        in_specs=(
            P("row", "col", None, None, None),
            P(None, "col", "row", None, None, None),
            P("row", "col", None, None, None),
        ),
        out_specs=P("row", "col", None, None, None),
        check_vma=False,
    )
```

profile of v0, /device:TPU:0, one launch (start us, length us, event | category | flops | bytes accessed | tf_op | source)
XLA Modules:
  0.0 394.5 jit_solution(15243626719083775768)
XLA Ops:
  6.5 0.7 all-gather.5.cloned.1.call-update
  7.3 0.7 all-gather.3.cloned.1.call-update
  8.0 0.7 copy.16
  8.7 118.3 %all-gather.5.cloned.1.call-done = f32[2,4,1,12,128,128]{5,4,3,2,1,0:T(8,128)} async-done(((f32[2,1,1,12,128,128]{5,4,3,2,1,0:T(8,128)}), f32[2,4,1,12,128,128]{5,4,3,2,1,0:T(8,128)}) %all-gather.5.cloned.1.call-update) | async-done | bytes 6291472 | tf_op jit(solution)/shard_map/all_gather | solution.py:32
  127.0 54.4 %all-gather.3.cloned.1.call-done = f32[8,1,16,128,128]{4,3,2,1,0:T(8,128)} async-done(((f32[1,1,16,128,128]{4,3,2,1,0:T(8,128)}), f32[8,1,16,128,128]{4,3,2,1,0:T(8,128)}) %all-gather.3.cloned.1.call-update) | async-done | bytes 8388624 | tf_op jit(solution)/shard_map/all_gather | solution.py:33
  181.3 0.1 broadcast_in_dim.38
  181.5 204.8 %while.19 = (s32[]{:T(128)}, f32[24,128,128]{2,0,1:T(8,128)S(1)}, s32[]{:T(128)}, s32[]{:T(128)}, s32[8,96,3]{1,2,0:T(4,128)S(1)}, /*index=5*/f32[8,1,16,128,128...) while((s32[]{:T(128)}, f32[24,128,128]{2,0,1:T(8,128)S(1)}, ...), condition=%wide.region_3.4_spmd, body=%wide.region_0.3_spmd.sunk | while | flops 2872450304 | bytes 57164012 | solution.py:49
  181.5 25.6 %conditional.2 = (f32[24,128,128]{2,0,1:T(8,128)S(1)}) conditional(s32[]{:T(128)} %convert_element_type.13, f32[24,128,128]{2,0,1:T(8,128)S(1)} %get-tuple-element.574, (s32[]{:T(128)}, s32[8,96,3]{1,2,0:T(4,128)S(1)}, s32[]{:T(128)}, f32[8,1,16,128,128]{4,3,2,1,0:T(8,128)}, f32[2,4,1,12,128,128]{5,4,3,2,1,0:T(8,128)}, ...), branch_computations={%region_1.1_spmd, %region_2.2_spmd} | conditional | flops 2872450304 | bytes 57163708 | solution.py:42
  181.5 1.2 dynamic-slice_bitcast_fusion.1
  182.8 3.5 gather_fusion.1
  186.3 1.3 dynamic-slice_bitcast_fusion
  187.6 3.6 gather_fusion
  191.2 9.5 %fusion.2 = f32[96,128,128]{2,1,0:T(8,128)S(1)} fusion(f32[96,128,128]{2,1,0:T(8,128)} %gather_fusion.1, f32[96,128,128]{2,1,0:T(8,128)} %gather_fusion, pred[96]{0:T(512)(128)(4,1)S(1)} %get-tuple-element.513, pred[96]{0:T(512)(128)(4,1)S(1)} %get-tuple-element.512), kind=kOutput, calls=%fused_computation.4 | convolution fusion | flops 2419064832 | bytes 18874560 | tf_op jit(solution)/shard_map/while/body/eval_jaxpr/cond/branch_1_fun/pik,pkj->pij/dot_general | solution.py:16
  200.8 6.3 %fusion.8 = f32[24,128,128]{2,0,1:T(8,128)S(1)} fusion(f32[24,128,128]{2,0,1:T(8,128)S(1)} %get-tuple-element.481, f32[96,128,128]{2,1,0:T(8,128)S(1)} %fusion.2, s32[96]{0:T(128)S(1)} %get-tuple-element.514, pred[96]{0:T(512)(128)(4,1)S(1)} %get-tuple-element.511), kind=kOutput, calls=%fused_computation.10 | convolution fusion | flops 453382656 | bytes 9437664 | tf_op jit(solution)/shard_map/while/body/eval_jaxpr/cond/branch_1_fun/op,pij->oij/dot_general | solution.py:21
  207.1 25.6 %conditional.2 = (f32[24,128,128]{2,0,1:T(8,128)S(1)}) conditional(s32[]{:T(128)} %convert_element_type.13, f32[24,128,128]{2,0,1:T(8,128)S(1)} %get-tuple-element.574, (s32[]{:T(128)}, s32[8,96,3]{1,2,0:T(4,128)S(1)}, s32[]{:T(128)}, f32[8,1,16,128,128]{4,3,2,1,0:T(8,128)}, f32[2,4,1,12,128,128]{5,4,3,2,1,0:T(8,128)}, ...), branch_computations={%region_1.1_spmd, %region_2.2_spmd} | conditional | flops 2872450304 | bytes 57163708 | solution.py:42
  207.1 1.2 dynamic-slice_bitcast_fusion.1
  208.4 3.5 gather_fusion.1
  211.9 1.3 dynamic-slice_bitcast_fusion
  213.2 3.6 gather_fusion
  216.8 9.5 %fusion.2 = f32[96,128,128]{2,1,0:T(8,128)S(1)} fusion(f32[96,128,128]{2,1,0:T(8,128)} %gather_fusion.1, f32[96,128,128]{2,1,0:T(8,128)} %gather_fusion, pred[96]{0:T(512)(128)(4,1)S(1)} %get-tuple-element.513, pred[96]{0:T(512)(128)(4,1)S(1)} %get-tuple-element.512), kind=kOutput, calls=%fused_computation.4 | convolution fusion | flops 2419064832 | bytes 18874560 | tf_op jit(solution)/shard_map/while/body/eval_jaxpr/cond/branch_1_fun/pik,pkj->pij/dot_general | solution.py:16
  226.4 6.3 %fusion.8 = f32[24,128,128]{2,0,1:T(8,128)S(1)} fusion(f32[24,128,128]{2,0,1:T(8,128)S(1)} %get-tuple-element.481, f32[96,128,128]{2,1,0:T(8,128)S(1)} %fusion.2, s32[96]{0:T(128)S(1)} %get-tuple-element.514, pred[96]{0:T(512)(128)(4,1)S(1)} %get-tuple-element.511), kind=kOutput, calls=%fused_computation.10 | convolution fusion | flops 453382656 | bytes 9437664 | tf_op jit(solution)/shard_map/while/body/eval_jaxpr/cond/branch_1_fun/op,pij->oij/dot_general | solution.py:21
  232.7 25.6 %conditional.2 = (f32[24,128,128]{2,0,1:T(8,128)S(1)}) conditional(s32[]{:T(128)} %convert_element_type.13, f32[24,128,128]{2,0,1:T(8,128)S(1)} %get-tuple-element.574, (s32[]{:T(128)}, s32[8,96,3]{1,2,0:T(4,128)S(1)}, s32[]{:T(128)}, f32[8,1,16,128,128]{4,3,2,1,0:T(8,128)}, f32[2,4,1,12,128,128]{5,4,3,2,1,0:T(8,128)}, ...), branch_computations={%region_1.1_spmd, %region_2.2_spmd} | conditional | flops 2872450304 | bytes 57163708 | solution.py:42
  232.7 1.2 dynamic-slice_bitcast_fusion.1
  234.0 3.5 gather_fusion.1
  237.5 1.3 dynamic-slice_bitcast_fusion
  238.8 3.6 gather_fusion
  242.4 9.5 %fusion.2 = f32[96,128,128]{2,1,0:T(8,128)S(1)} fusion(f32[96,128,128]{2,1,0:T(8,128)} %gather_fusion.1, f32[96,128,128]{2,1,0:T(8,128)} %gather_fusion, pred[96]{0:T(512)(128)(4,1)S(1)} %get-tuple-element.513, pred[96]{0:T(512)(128)(4,1)S(1)} %get-tuple-element.512), kind=kOutput, calls=%fused_computation.4 | convolution fusion | flops 2419064832 | bytes 18874560 | tf_op jit(solution)/shard_map/while/body/eval_jaxpr/cond/branch_1_fun/pik,pkj->pij/dot_general | solution.py:16
  252.0 6.3 %fusion.8 = f32[24,128,128]{2,0,1:T(8,128)S(1)} fusion(f32[24,128,128]{2,0,1:T(8,128)S(1)} %get-tuple-element.481, f32[96,128,128]{2,1,0:T(8,128)S(1)} %fusion.2, s32[96]{0:T(128)S(1)} %get-tuple-element.514, pred[96]{0:T(512)(128)(4,1)S(1)} %get-tuple-element.511), kind=kOutput, calls=%fused_computation.10 | convolution fusion | flops 453382656 | bytes 9437664 | tf_op jit(solution)/shard_map/while/body/eval_jaxpr/cond/branch_1_fun/op,pij->oij/dot_general | solution.py:21
  258.3 25.6 %conditional.2 = (f32[24,128,128]{2,0,1:T(8,128)S(1)}) conditional(s32[]{:T(128)} %convert_element_type.13, f32[24,128,128]{2,0,1:T(8,128)S(1)} %get-tuple-element.574, (s32[]{:T(128)}, s32[8,96,3]{1,2,0:T(4,128)S(1)}, s32[]{:T(128)}, f32[8,1,16,128,128]{4,3,2,1,0:T(8,128)}, f32[2,4,1,12,128,128]{5,4,3,2,1,0:T(8,128)}, ...), branch_computations={%region_1.1_spmd, %region_2.2_spmd} | conditional | flops 2872450304 | bytes 57163708 | solution.py:42
  258.3 1.2 dynamic-slice_bitcast_fusion.1
  259.6 3.5 gather_fusion.1
  263.1 1.3 dynamic-slice_bitcast_fusion
  264.4 3.6 gather_fusion
  268.0 9.5 %fusion.2 = f32[96,128,128]{2,1,0:T(8,128)S(1)} fusion(f32[96,128,128]{2,1,0:T(8,128)} %gather_fusion.1, f32[96,128,128]{2,1,0:T(8,128)} %gather_fusion, pred[96]{0:T(512)(128)(4,1)S(1)} %get-tuple-element.513, pred[96]{0:T(512)(128)(4,1)S(1)} %get-tuple-element.512), kind=kOutput, calls=%fused_computation.4 | convolution fusion | flops 2419064832 | bytes 18874560 | tf_op jit(solution)/shard_map/while/body/eval_jaxpr/cond/branch_1_fun/pik,pkj->pij/dot_general | solution.py:16
  277.6 6.3 %fusion.8 = f32[24,128,128]{2,0,1:T(8,128)S(1)} fusion(f32[24,128,128]{2,0,1:T(8,128)S(1)} %get-tuple-element.481, f32[96,128,128]{2,1,0:T(8,128)S(1)} %fusion.2, s32[96]{0:T(128)S(1)} %get-tuple-element.514, pred[96]{0:T(512)(128)(4,1)S(1)} %get-tuple-element.511), kind=kOutput, calls=%fused_computation.10 | convolution fusion | flops 453382656 | bytes 9437664 | tf_op jit(solution)/shard_map/while/body/eval_jaxpr/cond/branch_1_fun/op,pij->oij/dot_general | solution.py:21
  283.9 25.6 %conditional.2 = (f32[24,128,128]{2,0,1:T(8,128)S(1)}) conditional(s32[]{:T(128)} %convert_element_type.13, f32[24,128,128]{2,0,1:T(8,128)S(1)} %get-tuple-element.574, (s32[]{:T(128)}, s32[8,96,3]{1,2,0:T(4,128)S(1)}, s32[]{:T(128)}, f32[8,1,16,128,128]{4,3,2,1,0:T(8,128)}, f32[2,4,1,12,128,128]{5,4,3,2,1,0:T(8,128)}, ...), branch_computations={%region_1.1_spmd, %region_2.2_spmd} | conditional | flops 2872450304 | bytes 57163708 | solution.py:42
  283.9 1.2 dynamic-slice_bitcast_fusion.1
  285.2 3.5 gather_fusion.1
  288.7 1.3 dynamic-slice_bitcast_fusion
  290.0 3.6 gather_fusion
  293.6 9.5 %fusion.2 = f32[96,128,128]{2,1,0:T(8,128)S(1)} fusion(f32[96,128,128]{2,1,0:T(8,128)} %gather_fusion.1, f32[96,128,128]{2,1,0:T(8,128)} %gather_fusion, pred[96]{0:T(512)(128)(4,1)S(1)} %get-tuple-element.513, pred[96]{0:T(512)(128)(4,1)S(1)} %get-tuple-element.512), kind=kOutput, calls=%fused_computation.4 | convolution fusion | flops 2419064832 | bytes 18874560 | tf_op jit(solution)/shard_map/while/body/eval_jaxpr/cond/branch_1_fun/pik,pkj->pij/dot_general | solution.py:16
  303.2 6.3 %fusion.8 = f32[24,128,128]{2,0,1:T(8,128)S(1)} fusion(f32[24,128,128]{2,0,1:T(8,128)S(1)} %get-tuple-element.481, f32[96,128,128]{2,1,0:T(8,128)S(1)} %fusion.2, s32[96]{0:T(128)S(1)} %get-tuple-element.514, pred[96]{0:T(512)(128)(4,1)S(1)} %get-tuple-element.511), kind=kOutput, calls=%fused_computation.10 | convolution fusion | flops 453382656 | bytes 9437664 | tf_op jit(solution)/shard_map/while/body/eval_jaxpr/cond/branch_1_fun/op,pij->oij/dot_general | solution.py:21
  309.5 25.6 %conditional.2 = (f32[24,128,128]{2,0,1:T(8,128)S(1)}) conditional(s32[]{:T(128)} %convert_element_type.13, f32[24,128,128]{2,0,1:T(8,128)S(1)} %get-tuple-element.574, (s32[]{:T(128)}, s32[8,96,3]{1,2,0:T(4,128)S(1)}, s32[]{:T(128)}, f32[8,1,16,128,128]{4,3,2,1,0:T(8,128)}, f32[2,4,1,12,128,128]{5,4,3,2,1,0:T(8,128)}, ...), branch_computations={%region_1.1_spmd, %region_2.2_spmd} | conditional | flops 2872450304 | bytes 57163708 | solution.py:42
  309.5 1.2 dynamic-slice_bitcast_fusion.1
  310.8 3.5 gather_fusion.1
  314.3 1.3 dynamic-slice_bitcast_fusion
  315.6 3.6 gather_fusion
  319.2 9.5 %fusion.2 = f32[96,128,128]{2,1,0:T(8,128)S(1)} fusion(f32[96,128,128]{2,1,0:T(8,128)} %gather_fusion.1, f32[96,128,128]{2,1,0:T(8,128)} %gather_fusion, pred[96]{0:T(512)(128)(4,1)S(1)} %get-tuple-element.513, pred[96]{0:T(512)(128)(4,1)S(1)} %get-tuple-element.512), kind=kOutput, calls=%fused_computation.4 | convolution fusion | flops 2419064832 | bytes 18874560 | tf_op jit(solution)/shard_map/while/body/eval_jaxpr/cond/branch_1_fun/pik,pkj->pij/dot_general | solution.py:16
  328.8 6.3 %fusion.8 = f32[24,128,128]{2,0,1:T(8,128)S(1)} fusion(f32[24,128,128]{2,0,1:T(8,128)S(1)} %get-tuple-element.481, f32[96,128,128]{2,1,0:T(8,128)S(1)} %fusion.2, s32[96]{0:T(128)S(1)} %get-tuple-element.514, pred[96]{0:T(512)(128)(4,1)S(1)} %get-tuple-element.511), kind=kOutput, calls=%fused_computation.10 | convolution fusion | flops 453382656 | bytes 9437664 | tf_op jit(solution)/shard_map/while/body/eval_jaxpr/cond/branch_1_fun/op,pij->oij/dot_general | solution.py:21
  335.1 25.6 %conditional.2 = (f32[24,128,128]{2,0,1:T(8,128)S(1)}) conditional(s32[]{:T(128)} %convert_element_type.13, f32[24,128,128]{2,0,1:T(8,128)S(1)} %get-tuple-element.574, (s32[]{:T(128)}, s32[8,96,3]{1,2,0:T(4,128)S(1)}, s32[]{:T(128)}, f32[8,1,16,128,128]{4,3,2,1,0:T(8,128)}, f32[2,4,1,12,128,128]{5,4,3,2,1,0:T(8,128)}, ...), branch_computations={%region_1.1_spmd, %region_2.2_spmd} | conditional | flops 2872450304 | bytes 57163708 | solution.py:42
  335.1 1.2 dynamic-slice_bitcast_fusion.1
  336.4 3.5 gather_fusion.1
  339.9 1.3 dynamic-slice_bitcast_fusion
  341.2 3.6 gather_fusion
  344.8 9.5 %fusion.2 = f32[96,128,128]{2,1,0:T(8,128)S(1)} fusion(f32[96,128,128]{2,1,0:T(8,128)} %gather_fusion.1, f32[96,128,128]{2,1,0:T(8,128)} %gather_fusion, pred[96]{0:T(512)(128)(4,1)S(1)} %get-tuple-element.513, pred[96]{0:T(512)(128)(4,1)S(1)} %get-tuple-element.512), kind=kOutput, calls=%fused_computation.4 | convolution fusion | flops 2419064832 | bytes 18874560 | tf_op jit(solution)/shard_map/while/body/eval_jaxpr/cond/branch_1_fun/pik,pkj->pij/dot_general | solution.py:16
  354.4 6.3 %fusion.8 = f32[24,128,128]{2,0,1:T(8,128)S(1)} fusion(f32[24,128,128]{2,0,1:T(8,128)S(1)} %get-tuple-element.481, f32[96,128,128]{2,1,0:T(8,128)S(1)} %fusion.2, s32[96]{0:T(128)S(1)} %get-tuple-element.514, pred[96]{0:T(512)(128)(4,1)S(1)} %get-tuple-element.511), kind=kOutput, calls=%fused_computation.10 | convolution fusion | flops 453382656 | bytes 9437664 | tf_op jit(solution)/shard_map/while/body/eval_jaxpr/cond/branch_1_fun/op,pij->oij/dot_general | solution.py:21
  360.7 25.6 %conditional.2 = (f32[24,128,128]{2,0,1:T(8,128)S(1)}) conditional(s32[]{:T(128)} %convert_element_type.13, f32[24,128,128]{2,0,1:T(8,128)S(1)} %get-tuple-element.574, (s32[]{:T(128)}, s32[8,96,3]{1,2,0:T(4,128)S(1)}, s32[]{:T(128)}, f32[8,1,16,128,128]{4,3,2,1,0:T(8,128)}, f32[2,4,1,12,128,128]{5,4,3,2,1,0:T(8,128)}, ...), branch_computations={%region_1.1_spmd, %region_2.2_spmd} | conditional | flops 2872450304 | bytes 57163708 | solution.py:42
  360.7 1.2 dynamic-slice_bitcast_fusion.1
  362.0 3.5 gather_fusion.1
  365.5 1.3 dynamic-slice_bitcast_fusion
  366.8 3.6 gather_fusion
  370.4 9.5 %fusion.2 = f32[96,128,128]{2,1,0:T(8,128)S(1)} fusion(f32[96,128,128]{2,1,0:T(8,128)} %gather_fusion.1, f32[96,128,128]{2,1,0:T(8,128)} %gather_fusion, pred[96]{0:T(512)(128)(4,1)S(1)} %get-tuple-element.513, pred[96]{0:T(512)(128)(4,1)S(1)} %get-tuple-element.512), kind=kOutput, calls=%fused_computation.4 | convolution fusion | flops 2419064832 | bytes 18874560 | tf_op jit(solution)/shard_map/while/body/eval_jaxpr/cond/branch_1_fun/pik,pkj->pij/dot_general | solution.py:16
  380.0 6.3 %fusion.8 = f32[24,128,128]{2,0,1:T(8,128)S(1)} fusion(f32[24,128,128]{2,0,1:T(8,128)S(1)} %get-tuple-element.481, f32[96,128,128]{2,1,0:T(8,128)S(1)} %fusion.2, s32[96]{0:T(128)S(1)} %get-tuple-element.514, pred[96]{0:T(512)(128)(4,1)S(1)} %get-tuple-element.511), kind=kOutput, calls=%fused_computation.10 | convolution fusion | flops 453382656 | bytes 9437664 | tf_op jit(solution)/shard_map/while/body/eval_jaxpr/cond/branch_1_fun/op,pij->oij/dot_general | solution.py:21
  386.3 1.4 copy.15
  (34 shorter events, 0.3 us)
Async XLA Ops:
  6.5 120.4 %all-gather.5.cloned.1.call-start = ((), (), s32[]{:S(2)}) async-start(), calls=%async_computation.1 | async-start | bytes 7864320 | tf_op jit(solution)/shard_map/all_gather | solution.py:32
  7.3 174.1 %all-gather.3.cloned.1.call-start = ((), (), s32[]{:S(2)}) async-start(), calls=%async_computation | async-start | bytes 9437184 | tf_op jit(solution)/shard_map/all_gather | solution.py:33
Sparse Core Ops, SparseCore 0:
  8.9 118.0 all-gather.4
  128.9 52.4 all-gather.2
where the time goes:
time: 395 us
  waiting for transfers between devices  174 us (44%)
  matrix products  127 us (32%)
  local copies, waits for them, and re-layouts  79.3 us (20%)
  between operations  13.4 us (3%)
    all_gather x1, waiting for transfers between devices, shards(): right_all = lax.all_gather(right_panels, 'col', axis=1, tiled=True)  118 us
    dot_general x8, matrix products, contribute(): jnp.einsum('pik,pkj->pij', taken_left, taken_right, precision=lax.Precisi...  76.2 us
    all_gather x1, waiting for transfers between devices, shards(): pieces = lax.all_gather(left_panels, 'row', axis=0, tiled=True)  54.4 us
    dot_general x8, matrix products, contribute(): jnp.einsum('op,pij->oij', onehot, blocks, precision=lax.Precision.HIGHEST)  50.3 us
    gather x8, local copies, waits for them, and re-layouts, contribute(): taken_left = jnp.take(left_stack, left_slot, axis=0)  28.9 us
    gather x8, local copies, waits for them, and re-layouts, contribute(): taken_right = jnp.take(right_panel, right_slot, axis=0)  28.2 us
    squeeze x8, local copies, waits for them, and re-layouts, one_row(): left_stack = lax.dynamic_index_in_dim(pieces, offset, 0, keepdims=False)[0]  10.3 us
    squeeze x8, local copies, waits for them, and re-layouts, one_row(): right_panel = right_all[offset // col_count, offset % col_count, 0]  9.53 us
  transfers between devices with their start and end apart: 2, of which 2 were waited for; matrix products, arithmetic and copies ran while one was open for 0% of the time, Pallas kernels for 0%

commit v1 on v0

--- a/solution.py
+++ b/solution.py
@@ -29,7 +29,19 @@
     entries = product_lists[0, 0]
     step_count = entries.shape[0]
     running = jnp.zeros((OCAP, BLK, BLK), jnp.float32)
-    right_all = lax.all_gather(right_panels, "col", axis=1, tiled=True)
+    block_here = right_panels
+    u_next, all_rows, mixed_arr = (lax.psum(1, "col"), lax.axis_index("col"), block_here.shape[1])
+    runs = [ii * u_next if t == 1 else ii for t, ii in enumerate(block_here.shape)]
+    dd = 1
+    right_all = lax.dynamic_update_slice_in_dim(
+        jnp.zeros(runs, block_here.dtype), block_here, all_rows * mixed_arr, axis=1
+    )
+    while dd < u_next:
+        block_here = lax.ppermute(block_here, "col", [(t, (t + 1) % u_next) for t in range(u_next)])
+        right_all = lax.dynamic_update_slice_in_dim(
+            right_all, block_here, (all_rows - dd) % u_next * mixed_arr, axis=1
+        )
+        dd += 1
     pieces = lax.all_gather(left_panels, "row", axis=0, tiled=True)
 
     def one_row(offset, partial_value):

time: 395 us -> 338 us (0.86)
  waiting for transfers between devices: 174 us -> 102 us
  local copies, waits for them, and re-layouts: 79.3 us -> 90.9 us
    all_gather x1 -> x0, waiting for transfers between devices: 118 us -> none  [shards(): right_all = lax.all_gather(right_panels, 'col', axis=1, tiled=True)]
    ppermute x0 -> x3, waiting for transfers between devices: none -> 102 us  [shards(): lax.ppermute(block_here, 'col', [(t, (t + 1) % u_next) for t in range(u_n...]
    all_gather x1, waiting for transfers between devices: 54.4 us -> 0.01 us  [shards(): pieces = lax.all_gather(left_panels, 'row', axis=0, tiled=True)]
    dynamic_update_slice x0 -> x4, local copies, waits for them, and re-layouts: none -> 7.99 us  [the longest x3 6.72 us: shards(): lax.dynamic_update_slice_in_dim(right_all, block_here, (all_rows - dd) %...]
  transfers between devices with their start and end apart: 2 -> 4, of which waited for: 2 -> 3; matrix products, arithmetic and copies ran while one was open for 0% -> 4% of each run, Pallas kernels for 0% -> 0%
where the time goes in v1:
time: 338 us; the launch traced here: 337 us
  matrix products  127 us (38%)
  waiting for transfers between devices  102 us (30%)
  local copies, waits for them, and re-layouts  90.9 us (27%)
  between operations  13.4 us (4%)
    ppermute x3, waiting for transfers between devices, shards(): lax.ppermute(block_here, 'col', [(t, (t + 1) % u_next) for t in range(u_n...  102 us
    dot_general x8, matrix products, contribute(): jnp.einsum('pik,pkj->pij', taken_left, taken_right, precision=lax.Precisi...  76.2 us
    dot_general x8, matrix products, contribute(): jnp.einsum('op,pij->oij', onehot, blocks, precision=lax.Precision.HIGHEST)  50.3 us
    gather x8, local copies, waits for them, and re-layouts, contribute(): taken_right = jnp.take(right_panel, right_slot, axis=0)  29.1 us
    gather x8, local copies, waits for them, and re-layouts, contribute(): taken_left = jnp.take(left_stack, left_slot, axis=0)  28.2 us
    squeeze x8, local copies, waits for them, and re-layouts, one_row(): left_stack = lax.dynamic_index_in_dim(pieces, offset, 0, keepdims=False)[0]  10.3 us
    squeeze x8, local copies, waits for them, and re-layouts, one_row(): right_panel = right_all[offset // col_count, offset % col_count, 0]  9.53 us
  transfers between devices with their start and end apart: 4, of which 3 were waited for; matrix products, arithmetic and copies ran while one was open for 4% of the time, Pallas kernels for 0%

profile of v1, /device:TPU:0, one launch (start us, length us, event | category | flops | bytes accessed | tf_op | source)
XLA Modules:
  0.0 337.4 jit_solution(2619742474379782668)
XLA Ops:
  7.3 3.1 collective-permute-start
  10.4 36.6 %collective-permute-done = f32[2,1,1,12,128,128]{5,4,3,2,1,0:T(8,128)S(1)} collective-permute-done((f32[2,1,1,12,128,128]{5,4,3,2,1,0:T(8,128)}, f32[2,1,1,12,128,128]{5,4,3,2,1,0:T(8,128)S(1)}, u32[]{:S(2)}, u32[]{:S(2)}) %collective-permute-start) | collective-permute-done | bytes 1572896 | tf_op jit(solution)/shard_map/ppermute | solution.py:40
  47.0 37.5 %collective-permute-done.1 = f32[2,1,1,12,128,128]{5,4,3,2,1,0:T(8,128)} collective-permute-done((f32[2,1,1,12,128,128]{5,4,3,2,1,0:T(8,128)S(1)}, f32[2,1,1,12,128,128]{5,4,3,2,1,0:T(8,128)}, u32[]{:S(2)}, u32[]{:S(2)}) %collective-permute-start.1) | collective-permute-done | bytes 1572896 | tf_op jit(solution)/shard_map/ppermute | solution.py:40
  85.2 3.4 %broadcast_in_dim.42 = f32[2,4,1,12,128,128]{5,4,3,2,1,0:T(8,128)} broadcast(f32[]{:T(128)} %constant.226.clone.1), dimensions={} | broadcast | bytes 6291460 | tf_op jit(solution)/shard_map/broadcast_in_dim | solution.py:37
  88.6 1.3 constant_dynamic-update-slice_fusion.3
  89.9 1.2 constant_dynamic-update-slice_fusion.2
  91.1 2.7 constant_dynamic-update-slice_fusion.1
  93.8 27.4 %collective-permute-done.2 = f32[2,1,1,12,128,128]{5,4,3,2,1,0:T(8,128)} collective-permute-done((f32[2,1,1,12,128,128]{5,4,3,2,1,0:T(8,128)}, f32[2,1,1,12,128,128]{5,4,3,2,1,0:T(8,128)}, u32[]{:S(2)}, u32[]{:S(2)}) %collective-permute-start.2) | collective-permute-done | bytes 1572896 | tf_op jit(solution)/shard_map/ppermute | solution.py:40
  121.3 2.8 constant_dynamic-update-slice_fusion
  124.1 205.0 %while.19 = (s32[]{:T(128)}, f32[24,128,128]{2,0,1:T(8,128)S(1)}, s32[]{:T(128)}, s32[]{:T(128)}, s32[8,96,3]{1,2,0:T(4,128)S(1)}, /*index=5*/f32[8,1,16,128,128...) while((s32[]{:T(128)}, f32[24,128,128]{2,0,1:T(8,128)S(1)}, ...), condition=%wide.region_3.4_spmd, body=%wide.region_0.3_spmd.sunk | while | flops 2872450304 | bytes 57164012 | solution.py:61
  124.2 25.6 %conditional.2 = (f32[24,128,128]{2,0,1:T(8,128)S(1)}) conditional(s32[]{:T(128)} %convert_element_type.13, f32[24,128,128]{2,0,1:T(8,128)S(1)} %get-tuple-element.574, (s32[]{:T(128)}, s32[8,96,3]{1,2,0:T(4,128)S(1)}, s32[]{:T(128)}, f32[8,1,16,128,128]{4,3,2,1,0:T(8,128)}, f32[2,4,1,12,128,128]{5,4,3,2,1,0:T(8,128)}, ...), branch_computations={%region_1.1_spmd, %region_2.2_spmd} | conditional | flops 2872450304 | bytes 57163708 | solution.py:54
  124.2 1.2 dynamic-slice_bitcast_fusion.1
  125.5 3.6 %gather_fusion.1 = f32[96,128,128]{2,1,0:T(8,128)} fusion(f32[12,128,128]{2,1,0:T(8,128)S(1)} %dynamic-slice_bitcast_fusion.1, s32[1024]{0:T(1024)S(1)} %get-tuple-element.517), kind=kCustom, calls=%fused_computation.1 | custom fusion | bytes 12583296 | tf_op jit(solution)/shard_map/while/body/eval_jaxpr/cond/branch_1_fun/jit(_take)/gather | solution.py:15
  129.1 1.3 dynamic-slice_bitcast_fusion
  130.4 3.5 %gather_fusion = f32[96,128,128]{2,1,0:T(8,128)} fusion(f32[16,128,128]{2,1,0:T(8,128)S(1)} %dynamic-slice_bitcast_fusion, s32[1024]{0:T(1024)S(1)} %get-tuple-element.518), kind=kCustom, calls=%fused_computation | custom fusion | bytes 12583296 | tf_op jit(solution)/shard_map/while/body/eval_jaxpr/cond/branch_1_fun/jit(_take)/gather | solution.py:14
  133.9 9.5 %fusion.2 = f32[96,128,128]{2,1,0:T(8,128)S(1)} fusion(f32[96,128,128]{2,1,0:T(8,128)} %gather_fusion.1, f32[96,128,128]{2,1,0:T(8,128)} %gather_fusion, pred[96]{0:T(512)(128)(4,1)S(1)} %get-tuple-element.513, pred[96]{0:T(512)(128)(4,1)S(1)} %get-tuple-element.512), kind=kOutput, calls=%fused_computation.4 | convolution fusion | flops 2419064832 | bytes 18874560 | tf_op jit(solution)/shard_map/while/body/eval_jaxpr/cond/branch_1_fun/pik,pkj->pij/dot_general | solution.py:16
  143.5 6.3 %fusion.8 = f32[24,128,128]{2,0,1:T(8,128)S(1)} fusion(f32[24,128,128]{2,0,1:T(8,128)S(1)} %get-tuple-element.481, f32[96,128,128]{2,1,0:T(8,128)S(1)} %fusion.2, s32[96]{0:T(128)S(1)} %get-tuple-element.514, pred[96]{0:T(512)(128)(4,1)S(1)} %get-tuple-element.511), kind=kOutput, calls=%fused_computation.10 | convolution fusion | flops 453382656 | bytes 9437664 | tf_op jit(solution)/shard_map/while/body/eval_jaxpr/cond/branch_1_fun/op,pij->oij/dot_general | solution.py:21
  149.8 25.6 %conditional.2 = (f32[24,128,128]{2,0,1:T(8,128)S(1)}) conditional(s32[]{:T(128)} %convert_element_type.13, f32[24,128,128]{2,0,1:T(8,128)S(1)} %get-tuple-element.574, (s32[]{:T(128)}, s32[8,96,3]{1,2,0:T(4,128)S(1)}, s32[]{:T(128)}, f32[8,1,16,128,128]{4,3,2,1,0:T(8,128)}, f32[2,4,1,12,128,128]{5,4,3,2,1,0:T(8,128)}, ...), branch_computations={%region_1.1_spmd, %region_2.2_spmd} | conditional | flops 2872450304 | bytes 57163708 | solution.py:54
  149.8 1.2 dynamic-slice_bitcast_fusion.1
  151.1 3.6 %gather_fusion.1 = f32[96,128,128]{2,1,0:T(8,128)} fusion(f32[12,128,128]{2,1,0:T(8,128)S(1)} %dynamic-slice_bitcast_fusion.1, s32[1024]{0:T(1024)S(1)} %get-tuple-element.517), kind=kCustom, calls=%fused_computation.1 | custom fusion | bytes 12583296 | tf_op jit(solution)/shard_map/while/body/eval_jaxpr/cond/branch_1_fun/jit(_take)/gather | solution.py:15
  154.7 1.3 dynamic-slice_bitcast_fusion
  156.0 3.5 %gather_fusion = f32[96,128,128]{2,1,0:T(8,128)} fusion(f32[16,128,128]{2,1,0:T(8,128)S(1)} %dynamic-slice_bitcast_fusion, s32[1024]{0:T(1024)S(1)} %get-tuple-element.518), kind=kCustom, calls=%fused_computation | custom fusion | bytes 12583296 | tf_op jit(solution)/shard_map/while/body/eval_jaxpr/cond/branch_1_fun/jit(_take)/gather | solution.py:14
  159.6 9.5 %fusion.2 = f32[96,128,128]{2,1,0:T(8,128)S(1)} fusion(f32[96,128,128]{2,1,0:T(8,128)} %gather_fusion.1, f32[96,128,128]{2,1,0:T(8,128)} %gather_fusion, pred[96]{0:T(512)(128)(4,1)S(1)} %get-tuple-element.513, pred[96]{0:T(512)(128)(4,1)S(1)} %get-tuple-element.512), kind=kOutput, calls=%fused_computation.4 | convolution fusion | flops 2419064832 | bytes 18874560 | tf_op jit(solution)/shard_map/while/body/eval_jaxpr/cond/branch_1_fun/pik,pkj->pij/dot_general | solution.py:16
  169.1 6.3 %fusion.8 = f32[24,128,128]{2,0,1:T(8,128)S(1)} fusion(f32[24,128,128]{2,0,1:T(8,128)S(1)} %get-tuple-element.481, f32[96,128,128]{2,1,0:T(8,128)S(1)} %fusion.2, s32[96]{0:T(128)S(1)} %get-tuple-element.514, pred[96]{0:T(512)(128)(4,1)S(1)} %get-tuple-element.511), kind=kOutput, calls=%fused_computation.10 | convolution fusion | flops 453382656 | bytes 9437664 | tf_op jit(solution)/shard_map/while/body/eval_jaxpr/cond/branch_1_fun/op,pij->oij/dot_general | solution.py:21
  175.4 25.6 %conditional.2 = (f32[24,128,128]{2,0,1:T(8,128)S(1)}) conditional(s32[]{:T(128)} %convert_element_type.13, f32[24,128,128]{2,0,1:T(8,128)S(1)} %get-tuple-element.574, (s32[]{:T(128)}, s32[8,96,3]{1,2,0:T(4,128)S(1)}, s32[]{:T(128)}, f32[8,1,16,128,128]{4,3,2,1,0:T(8,128)}, f32[2,4,1,12,128,128]{5,4,3,2,1,0:T(8,128)}, ...), branch_computations={%region_1.1_spmd, %region_2.2_spmd} | conditional | flops 2872450304 | bytes 57163708 | solution.py:54
  175.5 1.2 dynamic-slice_bitcast_fusion.1
  176.7 3.6 %gather_fusion.1 = f32[96,128,128]{2,1,0:T(8,128)} fusion(f32[12,128,128]{2,1,0:T(8,128)S(1)} %dynamic-slice_bitcast_fusion.1, s32[1024]{0:T(1024)S(1)} %get-tuple-element.517), kind=kCustom, calls=%fused_computation.1 | custom fusion | bytes 12583296 | tf_op jit(solution)/shard_map/while/body/eval_jaxpr/cond/branch_1_fun/jit(_take)/gather | solution.py:15
  180.3 1.3 dynamic-slice_bitcast_fusion
  181.6 3.5 %gather_fusion = f32[96,128,128]{2,1,0:T(8,128)} fusion(f32[16,128,128]{2,1,0:T(8,128)S(1)} %dynamic-slice_bitcast_fusion, s32[1024]{0:T(1024)S(1)} %get-tuple-element.518), kind=kCustom, calls=%fused_computation | custom fusion | bytes 12583296 | tf_op jit(solution)/shard_map/while/body/eval_jaxpr/cond/branch_1_fun/jit(_take)/gather | solution.py:14
  185.2 9.5 %fusion.2 = f32[96,128,128]{2,1,0:T(8,128)S(1)} fusion(f32[96,128,128]{2,1,0:T(8,128)} %gather_fusion.1, f32[96,128,128]{2,1,0:T(8,128)} %gather_fusion, pred[96]{0:T(512)(128)(4,1)S(1)} %get-tuple-element.513, pred[96]{0:T(512)(128)(4,1)S(1)} %get-tuple-element.512), kind=kOutput, calls=%fused_computation.4 | convolution fusion | flops 2419064832 | bytes 18874560 | tf_op jit(solution)/shard_map/while/body/eval_jaxpr/cond/branch_1_fun/pik,pkj->pij/dot_general | solution.py:16
  194.7 6.3 %fusion.8 = f32[24,128,128]{2,0,1:T(8,128)S(1)} fusion(f32[24,128,128]{2,0,1:T(8,128)S(1)} %get-tuple-element.481, f32[96,128,128]{2,1,0:T(8,128)S(1)} %fusion.2, s32[96]{0:T(128)S(1)} %get-tuple-element.514, pred[96]{0:T(512)(128)(4,1)S(1)} %get-tuple-element.511), kind=kOutput, calls=%fused_computation.10 | convolution fusion | flops 453382656 | bytes 9437664 | tf_op jit(solution)/shard_map/while/body/eval_jaxpr/cond/branch_1_fun/op,pij->oij/dot_general | solution.py:21
  201.0 25.6 %conditional.2 = (f32[24,128,128]{2,0,1:T(8,128)S(1)}) conditional(s32[]{:T(128)} %convert_element_type.13, f32[24,128,128]{2,0,1:T(8,128)S(1)} %get-tuple-element.574, (s32[]{:T(128)}, s32[8,96,3]{1,2,0:T(4,128)S(1)}, s32[]{:T(128)}, f32[8,1,16,128,128]{4,3,2,1,0:T(8,128)}, f32[2,4,1,12,128,128]{5,4,3,2,1,0:T(8,128)}, ...), branch_computations={%region_1.1_spmd, %region_2.2_spmd} | conditional | flops 2872450304 | bytes 57163708 | solution.py:54
  202.3 3.6 %gather_fusion.1 = f32[96,128,128]{2,1,0:T(8,128)} fusion(f32[12,128,128]{2,1,0:T(8,128)S(1)} %dynamic-slice_bitcast_fusion.1, s32[1024]{0:T(1024)S(1)} %get-tuple-element.517), kind=kCustom, calls=%fused_computation.1 | custom fusion | bytes 12583296 | tf_op jit(solution)/shard_map/while/body/eval_jaxpr/cond/branch_1_fun/jit(_take)/gather | solution.py:15
  206.0 1.3 dynamic-slice_bitcast_fusion
  207.3 3.5 %gather_fusion = f32[96,128,128]{2,1,0:T(8,128)} fusion(f32[16,128,128]{2,1,0:T(8,128)S(1)} %dynamic-slice_bitcast_fusion, s32[1024]{0:T(1024)S(1)} %get-tuple-element.518), kind=kCustom, calls=%fused_computation | custom fusion | bytes 12583296 | tf_op jit(solution)/shard_map/while/body/eval_jaxpr/cond/branch_1_fun/jit(_take)/gather | solution.py:14
  210.8 9.5 %fusion.2 = f32[96,128,128]{2,1,0:T(8,128)S(1)} fusion(f32[96,128,128]{2,1,0:T(8,128)} %gather_fusion.1, f32[96,128,128]{2,1,0:T(8,128)} %gather_fusion, pred[96]{0:T(512)(128)(4,1)S(1)} %get-tuple-element.513, pred[96]{0:T(512)(128)(4,1)S(1)} %get-tuple-element.512), kind=kOutput, calls=%fused_computation.4 | convolution fusion | flops 2419064832 | bytes 18874560 | tf_op jit(solution)/shard_map/while/body/eval_jaxpr/cond/branch_1_fun/pik,pkj->pij/dot_general | solution.py:16
  220.3 6.3 %fusion.8 = f32[24,128,128]{2,0,1:T(8,128)S(1)} fusion(f32[24,128,128]{2,0,1:T(8,128)S(1)} %get-tuple-element.481, f32[96,128,128]{2,1,0:T(8,128)S(1)} %fusion.2, s32[96]{0:T(128)S(1)} %get-tuple-element.514, pred[96]{0:T(512)(128)(4,1)S(1)} %get-tuple-element.511), kind=kOutput, calls=%fused_computation.10 | convolution fusion | flops 453382656 | bytes 9437664 | tf_op jit(solution)/shard_map/while/body/eval_jaxpr/cond/branch_1_fun/op,pij->oij/dot_general | solution.py:21
  226.7 25.6 %conditional.2 = (f32[24,128,128]{2,0,1:T(8,128)S(1)}) conditional(s32[]{:T(128)} %convert_element_type.13, f32[24,128,128]{2,0,1:T(8,128)S(1)} %get-tuple-element.574, (s32[]{:T(128)}, s32[8,96,3]{1,2,0:T(4,128)S(1)}, s32[]{:T(128)}, f32[8,1,16,128,128]{4,3,2,1,0:T(8,128)}, f32[2,4,1,12,128,128]{5,4,3,2,1,0:T(8,128)}, ...), branch_computations={%region_1.1_spmd, %region_2.2_spmd} | conditional | flops 2872450304 | bytes 57163708 | solution.py:54
  228.0 3.6 %gather_fusion.1 = f32[96,128,128]{2,1,0:T(8,128)} fusion(f32[12,128,128]{2,1,0:T(8,128)S(1)} %dynamic-slice_bitcast_fusion.1, s32[1024]{0:T(1024)S(1)} %get-tuple-element.517), kind=kCustom, calls=%fused_computation.1 | custom fusion | bytes 12583296 | tf_op jit(solution)/shard_map/while/body/eval_jaxpr/cond/branch_1_fun/jit(_take)/gather | solution.py:15
  231.6 1.3 dynamic-slice_bitcast_fusion
  232.9 3.5 %gather_fusion = f32[96,128,128]{2,1,0:T(8,128)} fusion(f32[16,128,128]{2,1,0:T(8,128)S(1)} %dynamic-slice_bitcast_fusion, s32[1024]{0:T(1024)S(1)} %get-tuple-element.518), kind=kCustom, calls=%fused_computation | custom fusion | bytes 12583296 | tf_op jit(solution)/shard_map/while/body/eval_jaxpr/cond/branch_1_fun/jit(_take)/gather | solution.py:14
  236.4 9.5 %fusion.2 = f32[96,128,128]{2,1,0:T(8,128)S(1)} fusion(f32[96,128,128]{2,1,0:T(8,128)} %gather_fusion.1, f32[96,128,128]{2,1,0:T(8,128)} %gather_fusion, pred[96]{0:T(512)(128)(4,1)S(1)} %get-tuple-element.513, pred[96]{0:T(512)(128)(4,1)S(1)} %get-tuple-element.512), kind=kOutput, calls=%fused_computation.4 | convolution fusion | flops 2419064832 | bytes 18874560 | tf_op jit(solution)/shard_map/while/body/eval_jaxpr/cond/branch_1_fun/pik,pkj->pij/dot_general | solution.py:16
  246.0 6.3 %fusion.8 = f32[24,128,128]{2,0,1:T(8,128)S(1)} fusion(f32[24,128,128]{2,0,1:T(8,128)S(1)} %get-tuple-element.481, f32[96,128,128]{2,1,0:T(8,128)S(1)} %fusion.2, s32[96]{0:T(128)S(1)} %get-tuple-element.514, pred[96]{0:T(512)(128)(4,1)S(1)} %get-tuple-element.511), kind=kOutput, calls=%fused_computation.10 | convolution fusion | flops 453382656 | bytes 9437664 | tf_op jit(solution)/shard_map/while/body/eval_jaxpr/cond/branch_1_fun/op,pij->oij/dot_general | solution.py:21
  252.3 25.6 %conditional.2 = (f32[24,128,128]{2,0,1:T(8,128)S(1)}) conditional(s32[]{:T(128)} %convert_element_type.13, f32[24,128,128]{2,0,1:T(8,128)S(1)} %get-tuple-element.574, (s32[]{:T(128)}, s32[8,96,3]{1,2,0:T(4,128)S(1)}, s32[]{:T(128)}, f32[8,1,16,128,128]{4,3,2,1,0:T(8,128)}, f32[2,4,1,12,128,128]{5,4,3,2,1,0:T(8,128)}, ...), branch_computations={%region_1.1_spmd, %region_2.2_spmd} | conditional | flops 2872450304 | bytes 57163708 | solution.py:54
  252.3 1.2 dynamic-slice_bitcast_fusion.1
  253.6 3.6 %gather_fusion.1 = f32[96,128,128]{2,1,0:T(8,128)} fusion(f32[12,128,128]{2,1,0:T(8,128)S(1)} %dynamic-slice_bitcast_fusion.1, s32[1024]{0:T(1024)S(1)} %get-tuple-element.517), kind=kCustom, calls=%fused_computation.1 | custom fusion | bytes 12583296 | tf_op jit(solution)/shard_map/while/body/eval_jaxpr/cond/branch_1_fun/jit(_take)/gather | solution.py:15
  257.2 1.3 dynamic-slice_bitcast_fusion
  258.5 3.5 %gather_fusion = f32[96,128,128]{2,1,0:T(8,128)} fusion(f32[16,128,128]{2,1,0:T(8,128)S(1)} %dynamic-slice_bitcast_fusion, s32[1024]{0:T(1024)S(1)} %get-tuple-element.518), kind=kCustom, calls=%fused_computation | custom fusion | bytes 12583296 | tf_op jit(solution)/shard_map/while/body/eval_jaxpr/cond/branch_1_fun/jit(_take)/gather | solution.py:14
  262.0 9.5 %fusion.2 = f32[96,128,128]{2,1,0:T(8,128)S(1)} fusion(f32[96,128,128]{2,1,0:T(8,128)} %gather_fusion.1, f32[96,128,128]{2,1,0:T(8,128)} %gather_fusion, pred[96]{0:T(512)(128)(4,1)S(1)} %get-tuple-element.513, pred[96]{0:T(512)(128)(4,1)S(1)} %get-tuple-element.512), kind=kOutput, calls=%fused_computation.4 | convolution fusion | flops 2419064832 | bytes 18874560 | tf_op jit(solution)/shard_map/while/body/eval_jaxpr/cond/branch_1_fun/pik,pkj->pij/dot_general | solution.py:16
  271.6 6.3 %fusion.8 = f32[24,128,128]{2,0,1:T(8,128)S(1)} fusion(f32[24,128,128]{2,0,1:T(8,128)S(1)} %get-tuple-element.481, f32[96,128,128]{2,1,0:T(8,128)S(1)} %fusion.2, s32[96]{0:T(128)S(1)} %get-tuple-element.514, pred[96]{0:T(512)(128)(4,1)S(1)} %get-tuple-element.511), kind=kOutput, calls=%fused_computation.10 | convolution fusion | flops 453382656 | bytes 9437664 | tf_op jit(solution)/shard_map/while/body/eval_jaxpr/cond/branch_1_fun/op,pij->oij/dot_general | solution.py:21
  277.9 25.6 %conditional.2 = (f32[24,128,128]{2,0,1:T(8,128)S(1)}) conditional(s32[]{:T(128)} %convert_element_type.13, f32[24,128,128]{2,0,1:T(8,128)S(1)} %get-tuple-element.574, (s32[]{:T(128)}, s32[8,96,3]{1,2,0:T(4,128)S(1)}, s32[]{:T(128)}, f32[8,1,16,128,128]{4,3,2,1,0:T(8,128)}, f32[2,4,1,12,128,128]{5,4,3,2,1,0:T(8,128)}, ...), branch_computations={%region_1.1_spmd, %region_2.2_spmd} | conditional | flops 2872450304 | bytes 57163708 | solution.py:54
  279.2 3.6 %gather_fusion.1 = f32[96,128,128]{2,1,0:T(8,128)} fusion(f32[12,128,128]{2,1,0:T(8,128)S(1)} %dynamic-slice_bitcast_fusion.1, s32[1024]{0:T(1024)S(1)} %get-tuple-element.517), kind=kCustom, calls=%fused_computation.1 | custom fusion | bytes 12583296 | tf_op jit(solution)/shard_map/while/body/eval_jaxpr/cond/branch_1_fun/jit(_take)/gather | solution.py:15
  282.8 1.3 dynamic-slice_bitcast_fusion
  284.1 3.5 %gather_fusion = f32[96,128,128]{2,1,0:T(8,128)} fusion(f32[16,128,128]{2,1,0:T(8,128)S(1)} %dynamic-slice_bitcast_fusion, s32[1024]{0:T(1024)S(1)} %get-tuple-element.518), kind=kCustom, calls=%fused_computation | custom fusion | bytes 12583296 | tf_op jit(solution)/shard_map/while/body/eval_jaxpr/cond/branch_1_fun/jit(_take)/gather | solution.py:14
  287.7 9.5 %fusion.2 = f32[96,128,128]{2,1,0:T(8,128)S(1)} fusion(f32[96,128,128]{2,1,0:T(8,128)} %gather_fusion.1, f32[96,128,128]{2,1,0:T(8,128)} %gather_fusion, pred[96]{0:T(512)(128)(4,1)S(1)} %get-tuple-element.513, pred[96]{0:T(512)(128)(4,1)S(1)} %get-tuple-element.512), kind=kOutput, calls=%fused_computation.4 | convolution fusion | flops 2419064832 | bytes 18874560 | tf_op jit(solution)/shard_map/while/body/eval_jaxpr/cond/branch_1_fun/pik,pkj->pij/dot_general | solution.py:16
  297.2 6.3 %fusion.8 = f32[24,128,128]{2,0,1:T(8,128)S(1)} fusion(f32[24,128,128]{2,0,1:T(8,128)S(1)} %get-tuple-element.481, f32[96,128,128]{2,1,0:T(8,128)S(1)} %fusion.2, s32[96]{0:T(128)S(1)} %get-tuple-element.514, pred[96]{0:T(512)(128)(4,1)S(1)} %get-tuple-element.511), kind=kOutput, calls=%fused_computation.10 | convolution fusion | flops 453382656 | bytes 9437664 | tf_op jit(solution)/shard_map/while/body/eval_jaxpr/cond/branch_1_fun/op,pij->oij/dot_general | solution.py:21
  303.5 25.6 %conditional.2 = (f32[24,128,128]{2,0,1:T(8,128)S(1)}) conditional(s32[]{:T(128)} %convert_element_type.13, f32[24,128,128]{2,0,1:T(8,128)S(1)} %get-tuple-element.574, (s32[]{:T(128)}, s32[8,96,3]{1,2,0:T(4,128)S(1)}, s32[]{:T(128)}, f32[8,1,16,128,128]{4,3,2,1,0:T(8,128)}, f32[2,4,1,12,128,128]{5,4,3,2,1,0:T(8,128)}, ...), branch_computations={%region_1.1_spmd, %region_2.2_spmd} | conditional | flops 2872450304 | bytes 57163708 | solution.py:54
  303.6 1.2 dynamic-slice_bitcast_fusion.1
  304.8 3.6 %gather_fusion.1 = f32[96,128,128]{2,1,0:T(8,128)} fusion(f32[12,128,128]{2,1,0:T(8,128)S(1)} %dynamic-slice_bitcast_fusion.1, s32[1024]{0:T(1024)S(1)} %get-tuple-element.517), kind=kCustom, calls=%fused_computation.1 | custom fusion | bytes 12583296 | tf_op jit(solution)/shard_map/while/body/eval_jaxpr/cond/branch_1_fun/jit(_take)/gather | solution.py:15
  308.5 1.3 dynamic-slice_bitcast_fusion
  309.8 3.5 %gather_fusion = f32[96,128,128]{2,1,0:T(8,128)} fusion(f32[16,128,128]{2,1,0:T(8,128)S(1)} %dynamic-slice_bitcast_fusion, s32[1024]{0:T(1024)S(1)} %get-tuple-element.518), kind=kCustom, calls=%fused_computation | custom fusion | bytes 12583296 | tf_op jit(solution)/shard_map/while/body/eval_jaxpr/cond/branch_1_fun/jit(_take)/gather | solution.py:14
  313.3 9.5 %fusion.2 = f32[96,128,128]{2,1,0:T(8,128)S(1)} fusion(f32[96,128,128]{2,1,0:T(8,128)} %gather_fusion.1, f32[96,128,128]{2,1,0:T(8,128)} %gather_fusion, pred[96]{0:T(512)(128)(4,1)S(1)} %get-tuple-element.513, pred[96]{0:T(512)(128)(4,1)S(1)} %get-tuple-element.512), kind=kOutput, calls=%fused_computation.4 | convolution fusion | flops 2419064832 | bytes 18874560 | tf_op jit(solution)/shard_map/while/body/eval_jaxpr/cond/branch_1_fun/pik,pkj->pij/dot_general | solution.py:16
  322.8 6.3 %fusion.8 = f32[24,128,128]{2,0,1:T(8,128)S(1)} fusion(f32[24,128,128]{2,0,1:T(8,128)S(1)} %get-tuple-element.481, f32[96,128,128]{2,1,0:T(8,128)S(1)} %fusion.2, s32[96]{0:T(128)S(1)} %get-tuple-element.514, pred[96]{0:T(512)(128)(4,1)S(1)} %get-tuple-element.511), kind=kOutput, calls=%fused_computation.10 | convolution fusion | flops 453382656 | bytes 9437664 | tf_op jit(solution)/shard_map/while/body/eval_jaxpr/cond/branch_1_fun/op,pij->oij/dot_general | solution.py:21
  329.1 1.4 copy.15
  (44 shorter events, 5.3 us)
Async XLA Ops:
  6.5 82.1 %copy-start = (f32[2,1,1,12,128,128]{5,4,3,2,1,0:T(8,128)S(1)}, f32[2,1,1,12,128,128]{5,4,3,2,1,0:T(8,128)}, u32[]{:S(2)}) copy-start(f32[2,1,1,12,128,128]{5,4,3,2,1,0:T(8,128)} %param.8) | copy-start | bytes 4718596
  6.5 117.5 %all-gather.2.cloned.1.call-start = ((), (), s32[]{:S(2)}) async-start(), calls=%async_computation | async-start | bytes 9437184 | tf_op jit(solution)/shard_map/all_gather | solution.py:45
  7.3 39.7 %collective-permute-start = (f32[2,1,1,12,128,128]{5,4,3,2,1,0:T(8,128)}, f32[2,1,1,12,128,128]{5,4,3,2,1,0:T(8,128)S(1)}, u32[]{:S(2)}, u32[]{:S(2)}) collective-permute-start(f32[2,1,1,12,128,128]{5,4,3,2,1,0:T(8,128)} %param.8), channel_id=1, source_target_pairs={{0,1},{1,2},{2,3},{3,0},{4,5},{5,6},{6,7},{7,4},{8,9},{9,10},{10,1... | collective-permute-start | bytes 4718600 | tf_op jit(solution)/shard_map/ppermute | solution.py:40
  47.0 37.5 %collective-permute-start.1 = (f32[2,1,1,12,128,128]{5,4,3,2,1,0:T(8,128)S(1)}, f32[2,1,1,12,128,128]{5,4,3,2,1,0:T(8,128)}, u32[]{:S(2)}, u32[]{:S(2)}) collective-permute-start(f32[2,1,1,12,128,128]{5,4,3,2,1,0:T(8,128)S(1)} %collective-permute-done), channel_id=1, source_target_pairs={{0,1},{1,2},{2,3},{3,0},{4,5},{5,6},{6,7},{7,4},{8,9},{9,10},{10,1... | collective-permute-start | bytes 4718600 | tf_op jit(solution)/shard_map/ppermute | solution.py:40
  84.5 36.8 %collective-permute-start.2 = (f32[2,1,1,12,128,128]{5,4,3,2,1,0:T(8,128)}, f32[2,1,1,12,128,128]{5,4,3,2,1,0:T(8,128)}, u32[]{:S(2)}, u32[]{:S(2)}) collective-permute-start(f32[2,1,1,12,128,128]{5,4,3,2,1,0:T(8,128)} %collective-permute-done.1), channel_id=1, source_target_pairs={{0,1},{1,2},{2,3},{3,0},{4,5},{5,6},{6,7},{7,4},{8,9},{9,10},{10,1... | collective-permute-start | bytes 4718600 | tf_op jit(solution)/shard_map/ppermute | solution.py:40
Sparse Core Ops, SparseCore 0:
  9.2 56.9 all-gather.1
